TPU v7x, 512 devices: a whole 4x8x8 slice. The times are simulated.
512 devices in a mesh: station: 32 (over y, x), tm: 16 (over z, core).
Axes of the slice: x: 4, y: 8, z: 8, core: 2. Of those that a mesh axis runs over, the one named last changes fastest.
Arguments:
- spectra: bfloat16 [16, 128, 4096], P('tm', 'station'), may hold values from -5 to 5
- valid: int32 [16, 128], P('tm', 'station'), may hold values from 0 to 1, as said below
- pair_blocks: int32 [32, 17], P('station'), may hold values from 0 to 31, as said below
Outputs:
- correlations: float32 [8704, 512], P(('station', 'tm'))
Inputs may be any that keep to these rules, and one draw needn't show every extreme that they name: `pair_blocks`: row d begins with d, its 17 entries are distinct, and every unordered pair of blocks appears in some row. `valid`: each station misses one cyclic run of 1 to 7 hours.
All inputs are finite; a program needn't handle non-finite values.
Results may differ from a plain program's by a relative error of at most 0.0026.
Values may be sent and summed in bfloat16 or wider, within the bound.
A program may use at most 64 MiB of HBM per device.

v0:
```python
import math
import jax
import jax.numpy as jnp
from jax import lax
from jax.sharding import PartitionSpec as P

LAGS = 512


def make_lag_table(half_width, lag_count):
    bins = jnp.arange(half_width, dtype=jnp.int32)
    shifts = jnp.arange(lag_count, dtype=jnp.int32) - lag_count // 2
    phase = (2 * bins[:, None] + 1) * shifts[None, :] % (4 * half_width)
    angle = phase.astype(jnp.float32) * (math.pi / (2.0 * half_width))
    return jnp.concatenate([jnp.cos(angle), -jnp.sin(angle)], axis=0).astype(jnp.bfloat16)


def cross_stack(own_block, partner_block, half_width):
    own_real, own_imag = (own_block[..., :half_width], own_block[..., half_width:])
    part_real, part_imag = (partner_block[..., :half_width], partner_block[..., half_width:])
    cross_real = jnp.einsum(
        "haf,hkbf->kabf", own_real, part_real, preferred_element_type=jnp.float32
    ) + jnp.einsum("haf,hkbf->kabf", own_imag, part_imag, preferred_element_type=jnp.float32)
    cross_imag = jnp.einsum(
        "haf,hkbf->kabf", own_imag, part_real, preferred_element_type=jnp.float32
    ) - jnp.einsum("haf,hkbf->kabf", own_real, part_imag, preferred_element_type=jnp.float32)
    return jnp.concatenate([cross_real, cross_imag], axis=-1).astype(jnp.bfloat16)


def per_device(spectra, valid, pair_blocks):
    local_hours, block_len, spec_width = spectra.shape
    half_width = spec_width // 2
    lag_count = LAGS
    stations_axis = lax.axis_size("station")
    slot_count = pair_blocks.shape[1]
    plan = pair_blocks[0]
    masked = spectra * valid[:, :, None].astype(jnp.bfloat16)
    gathered, gathered_flags = (
        lax.all_gather(masked, "station", axis=1, tiled=True),
        lax.all_gather(valid, "station", axis=1, tiled=True),
    )
    gathered = gathered.reshape(local_hours, stations_axis, block_len, spec_width)
    gathered_flags = gathered_flags.reshape(local_hours, stations_axis, block_len)
    partners = jnp.take(gathered, plan, axis=1)
    partner_flags = jnp.take(gathered_flags, plan, axis=1)
    per_slot = block_len * block_len
    pair_count = slot_count * per_slot
    lag_table = make_lag_table(half_width, lag_count)
    stacked = cross_stack(masked, partners, half_width).reshape(pair_count, spec_width)
    partial_value = jnp.dot(stacked, lag_table, preferred_element_type=jnp.float32)
    local_counts = jnp.einsum(
        "ha,hkb->kab", valid.astype(jnp.float32), partner_flags.astype(jnp.float32)
    ).reshape(pair_count)
    summed, counts = (
        lax.psum_scatter(partial_value, "tm", scatter_dimension=0, tiled=True),
        lax.psum_scatter(local_counts, "tm", scatter_dimension=0, tiled=True),
    )
    lag_scale = 4.0 / math.sqrt(half_width)
    return summed * lag_scale / counts[:, None]


def solution(mesh):
    placed = (P("tm", "station", None), P("tm", "station"), P("station", None))
    return jax.shard_map(
        per_device,
        mesh=mesh,
        in_specs=placed,
        out_specs=P(("station", "tm"), None),
        check_vma=False,
    )
```

profile of v0, /device:TPU:1, one launch (start us, length us, event | category | flops | bytes accessed | tf_op | source)
XLA Modules:
  0.0 195.7 jit_solution(14837320123272706570)
XLA Ops:
  6.5 0.7 convert_bitcast_fusion.2
  7.3 1.5 copy_multiply_fusion
  8.8 0.7 compare_and_fusion
  9.5 0.7 fusion.16
  10.1 1.3 dynamic-slice
  12.1 0.8 bitcast_dynamic-update-slice_fusion
  12.8 17.5 %all-reduce = s32[128]{0:T(128)S(1)} all-reduce(s32[128]{0:T(128)S(1)} %bitcast_dynamic-update-slice_fusion), channel_id=1, replica_groups=mesh['station'=32,'tm'=16] {'station'}, use_global_device_ids=true, to_apply=%add | all-reduce | flops 128 | bytes 1024
  30.4 0.6 gather_fusion.1
  31.2 0.8 slice_convert_fusion.1
  32.0 19.2 %cosine_convert_fusion = (bf16[2048,512]{1,0:T(8,128)(2,1)}, bf16[2048,512]{1,0:T(8,128)(2,1)}) fusion(s32[512]{0:T(512)S(1)} %iota_add_fusion, s32[2048]{0:T(1024)S(1)} %multiply_add_fusion), kind=kLoop, calls=%fused_computation.15 | loop fusion | flops 17825792 | bytes 4204544 | tf_op jit(solution)/shard_map/convert.24
  51.2 44.4 %all-gather.2.cloned.1.call-done = bf16[1,128,4096]{2,0,1:T(2,128)(2,1)} async-done(((bf16[1,4,4096]{2,0,1:T(2,128)(2,1)}), bf16[1,128,4096]{2,0,1:T(2,128)(2,1)}) %all-gather.2.cloned.1.call-update) | async-done | bytes 1048592 | tf_op jit(solution)/shard_map/all_gather | solution.py:39
  95.6 7.7 %reduce = bf16[128,4096]{1,0:T(8,128)(2,1)S(1)} reduce(bf16[1,128,4096]{2,0,1:T(2,128)(2,1)} %all-gather.2.cloned.1.call-done, bf16[]{:T(256)} %constant.71), dimensions={0}, to_apply=%all_gather.6.reduce_sub_computation | reduce | bytes 2097154 | tf_op jit(solution)/shard_map/all_gather | solution.py:39
  103.3 0.4 reshape.161
  103.8 1.0 gather_fusion
  104.8 0.3 bitcast_select_fusion
  105.1 0.1 convert_bitcast_fusion.1
  105.2 1.2 fusion.11
  106.4 1.2 concatenate.13
  107.6 1.1 concatenate.14
  108.7 0.9 copy-done
  109.6 3.6 %fusion.4 = f32[272,512]{1,0:T(8,128)S(1)} fusion(bf16[2048,512]{1,0:T(8,128)(2,1)} %get-tuple-element.12, bf16[2048,512]{1,0:T(8,128)(2,1)S(1)} %copy-done, bf16[272,2048]{1,0:T(8,128)(2,1)} %concatenate.14, bf16[272,2048]{1,0:T(8,128)(2,1)} %concatenate.13), kind=kOutput, calls=%fused_computation.10 | convolution fusion | flops 1153695744 | bytes 6979584 | tf_op jit(solution)/shard_map/dot_general | solution.py:50
  113.2 32.3 %fusion = f32[24,512]{1,0:T(8,128)S(1)} fusion(f32[272,512]{1,0:T(8,128)S(1)} %fusion.4), kind=kCustom, calls=%all-reduce-scatter | all-reduce-scatter fusion | flops 196609 | bytes 608256
  145.5 1.5 collective-permute-start.3
  146.9 9.1 %collective-permute-start.2 = (f32[24,512]{1,0:T(8,128)S(1)}, f32[24,512]{1,0:T(8,128)S(1)}, u32[]{:S(2)}, u32[]{:S(2)}) collective-permute-start(f32[24,512]{1,0:T(8,128)S(1)} %fusion), channel_id=1, source_target_pairs={{0,3},{1,4},{2,5},{3,6},{4,7},{5,8},{6,9},{7,10},{8,11},{9,12},{10... | collective-permute-start | bytes 147464
  156.0 1.3 collective-permute-start.1
  157.3 3.1 %collective-permute-start = (f32[24,512]{1,0:T(8,128)S(1)}, f32[24,512]{1,0:T(8,128)S(1)}, u32[]{:S(2)}, u32[]{:S(2)}) collective-permute-start(f32[24,512]{1,0:T(8,128)S(1)} %fusion), channel_id=1, source_target_pairs={{0,1},{1,2},{2,3},{3,4},{4,5},{5,6},{6,7},{7,8},{8,9},{9,10},{10,1... | collective-permute-start | bytes 147464
  160.4 1.4 collective-permute-start.4
  161.8 0.1 reshape.156
  162.0 0.6 fusion.18
  163.8 23.6 %all-reduce.2 = f32[272]{0:T(512)S(1)} all-reduce(f32[272]{0:T(512)S(1)} %reshape.156), channel_id=3, replica_groups=mesh['station'=32,'tm'=16] {'tm'}, use_global_device_ids=true, to_apply=%region_1.2.clone | all-reduce | flops 272 | bytes 2176
  187.5 0.7 concatenate.17
  188.2 0.7 fusion.13
  (22 shorter events, 0.5 us)
Async XLA Ops:
  6.5 89.0 %all-gather.2.cloned.1.call-start = ((), (), s32[]{:S(2)}) async-start(), calls=%async_computation | async-start | bytes 2162688 | tf_op jit(solution)/shard_map/all_gather | solution.py:39
  107.6 2.0 %copy-start = (bf16[2048,512]{1,0:T(8,128)(2,1)S(1)}, bf16[2048,512]{1,0:T(8,128)(2,1)}, u32[]{:S(2)}) copy-start(bf16[2048,512]{1,0:T(8,128)(2,1)} %get-tuple-element.11) | copy-start | bytes 6291460
  109.6 52.4 %copy-start.1 = (u32[512]{0:T(512)S(1)}, u32[512]{0:T(512)}, u32[]{:S(2)}) copy-start(u32[512]{0:T(512)} %constant.65) | copy-start | bytes 6148
  145.5 42.0 %collective-permute-start.3 = (f32[24,512]{1,0:T(8,128)S(1)}, f32[24,512]{1,0:T(8,128)S(1)}, u32[]{:S(2)}, u32[]{:S(2)}) collective-permute-start(f32[24,512]{1,0:T(8,128)S(1)} %fusion), channel_id=1, source_target_pairs={{0,4},{1,5},{2,6},{3,7},{4,8},{5,9},{6,10},{7,11},{8,12},{9,13},{1... | collective-permute-start | bytes 147464
  146.9 40.5 %collective-permute-start.2 = (f32[24,512]{1,0:T(8,128)S(1)}, f32[24,512]{1,0:T(8,128)S(1)}, u32[]{:S(2)}, u32[]{:S(2)}) collective-permute-start(f32[24,512]{1,0:T(8,128)S(1)} %fusion), channel_id=1, source_target_pairs={{0,3},{1,4},{2,5},{3,6},{4,7},{5,8},{6,9},{7,10},{8,11},{9,12},{10... | collective-permute-start | bytes 147464
  156.0 31.5 %collective-permute-start.1 = (f32[24,512]{1,0:T(8,128)S(1)}, f32[24,512]{1,0:T(8,128)S(1)}, u32[]{:S(2)}, u32[]{:S(2)}) collective-permute-start(f32[24,512]{1,0:T(8,128)S(1)} %fusion), channel_id=1, source_target_pairs={{0,2},{1,3},{2,4},{3,5},{4,6},{5,7},{6,8},{7,9},{8,10},{9,11},{10,... | collective-permute-start | bytes 147464
  157.3 30.2 %collective-permute-start = (f32[24,512]{1,0:T(8,128)S(1)}, f32[24,512]{1,0:T(8,128)S(1)}, u32[]{:S(2)}, u32[]{:S(2)}) collective-permute-start(f32[24,512]{1,0:T(8,128)S(1)} %fusion), channel_id=1, source_target_pairs={{0,1},{1,2},{2,3},{3,4},{4,5},{5,6},{6,7},{7,8},{8,9},{9,10},{10,1... | collective-permute-start | bytes 147464
  160.4 27.0 %collective-permute-start.4 = (f32[9,512]{1,0:T(8,128)S(1)}, f32[9,512]{1,0:T(8,128)S(1)}, u32[]{:S(2)}, u32[]{:S(2)}) collective-permute-start(f32[9,512]{1,0:T(8,128)S(1)} %slice.24), channel_id=1, source_target_pairs={{0,5},{1,6},{2,7},{3,8},{4,9},{5,10},{6,11},{7,12},{8,13},{9,14},{... | collective-permute-start | bytes 55304
Sparse Core Ops, SparseCore 0:
  10.5 85.0 all-gather.1
where the time goes:
time: 196 us
  blocking collectives  73.3 us (37%)
  waiting for transfers between devices  44.4 us (23%)
  other arithmetic  33.7 us (17%)
  starting transfers between devices  16.3 us (8%)
  between operations  15.5 us (8%)
  local copies, waits for them, and re-layouts  9.01 us (5%)
  matrix products  3.59 us (2%)
    unnamed x3, blocking collectives  73.3 us
    all_gather x1, waiting for transfers between devices, per_device(): lax.all_gather(masked, 'station', axis=1, tiled=True)  44.4 us
    another operation x4, other arithmetic  20.9 us
    unnamed x5, starting transfers between devices  16.3 us
    all_gather x1, other arithmetic, per_device(): lax.all_gather(masked, 'station', axis=1, tiled=True)  7.73 us
    unnamed x11, local copies, waits for them, and re-layouts  4.29 us
  transfers between devices with their start and end apart: 6, of which 1 were waited for; matrix products, arithmetic and copies ran while one was open for 13% of the time, Pallas kernels for 0%

commit v1 on v0

--- a/solution.py
+++ b/solution.py
@@ -35,8 +35,17 @@
     slot_count = pair_blocks.shape[1]
     plan = pair_blocks[0]
     masked = spectra * valid[:, :, None].astype(jnp.bfloat16)
+
+    def refer_the_cells(shard_in):
+        axis_key = "station"
+        num = jax.lax.axis_size(axis_key)
+        state_next = jnp.tile(
+            shard_in, [num if dev_j == 1 else 1 for dev_j in range(shard_in.ndim)]
+        )
+        return jax.lax.all_to_all(state_next, axis_key, split_axis=1, concat_axis=1, tiled=True)
+
     gathered, gathered_flags = (
-        lax.all_gather(masked, "station", axis=1, tiled=True),
+        refer_the_cells(masked),
         lax.all_gather(valid, "station", axis=1, tiled=True),
     )
     gathered = gathered.reshape(local_hours, stations_axis, block_len, spec_width)

time: 196 us -> 169 us (0.86)
  waiting for transfers between devices: 44.4 us -> 0.02 us
  blocking collectives: 73.3 us -> 87.5 us
  between operations: 15.5 us -> 2.23 us
  local copies, waits for them, and re-layouts: 9.01 us -> 19.8 us
  starting transfers between devices: 16.3 us -> 24.9 us
  other arithmetic: 33.7 us -> 30.3 us
    all_gather x1 -> x0, waiting for transfers between devices: 44.4 us -> none  [per_device(): lax.all_gather(masked, 'station', axis=1, tiled=True)]
    unnamed x3, blocking collectives: 73.3 us -> 87.5 us
    all_to_all x0 -> x1, starting transfers between devices: none -> 10.5 us  [refer_the_cells(): jax.lax.all_to_all(state_next, axis_key, split_axis=1, concat_axis=1, til...]
    all_gather x1 -> x0, other arithmetic: 7.73 us -> none  [per_device(): lax.all_gather(masked, 'station', axis=1, tiled=True)]
    unnamed x0 -> x1, other arithmetic: none -> 7.02 us
    all_to_all x0 -> x1, local copies, waits for them, and re-layouts: none -> 6.21 us  [refer_the_cells(): jax.lax.all_to_all(state_next, axis_key, split_axis=1, concat_axis=1, til...]
    unnamed x11 -> x20, local copies, waits for them, and re-layouts: 4.29 us -> 6.9 us
    another operation x1 -> x2, local copies, waits for them, and re-layouts: 0.03 us -> 2.01 us  [refer_the_cells(): jnp.tile(shard_in, [num if dev_j == 1 else 1 for dev_j in range(shard_in....]
  transfers between devices with their start and end apart: 6 -> 6, of which waited for: 1 -> 0; matrix products, arithmetic and copies ran while one was open for 13% -> 13% of each run, Pallas kernels for 0% -> 0%
where the time goes in v1:
time: 169 us; the launch traced here: 168 us
  blocking collectives  87.5 us (52%)
  other arithmetic  30.3 us (18%)
  starting transfers between devices  24.9 us (15%)
  local copies, waits for them, and re-layouts  19.8 us (12%)
  matrix products  3.59 us (2%)
  between operations  2.23 us (1%)
    unnamed x3, blocking collectives  87.5 us
    another operation x4, other arithmetic  20 us
    unnamed x5, starting transfers between devices  14.4 us
    all_to_all x1, starting transfers between devices, refer_the_cells(): jax.lax.all_to_all(state_next, axis_key, split_axis=1, concat_axis=1, til...  10.5 us
    unnamed x1, other arithmetic  7.02 us
    unnamed x20, local copies, waits for them, and re-layouts  6.9 us
    all_to_all x1, local copies, waits for them, and re-layouts, refer_the_cells(): jax.lax.all_to_all(state_next, axis_key, split_axis=1, concat_axis=1, til...  6.21 us
    dot_general x1, matrix products, per_device(): jnp.dot(stacked, lag_table, preferred_element_type=jnp.float32)  3.59 us
  transfers between devices with their start and end apart: 6, of which 0 were waited for; matrix products, arithmetic and copies ran while one was open for 13% of the time, Pallas kernels for 0%

profile of v1, /device:TPU:1, one launch (start us, length us, event | category | flops | bytes accessed | tf_op | source)
XLA Modules:
  0.0 168.3 jit_solution(15026225264998155883)
XLA Ops:
  0.0 0.7 convert_bitcast_fusion.4
  0.7 0.8 fusion.19
  1.6 0.5 tile.12
  2.1 1.5 tile.14
  3.6 0.5 broadcast.142
  4.1 7.0 %reduce.2 = bf16[128,4096]{1,0:T(8,128)(2,1)S(1)} reduce(bf16[128,1,4096]{2,1,0:T(2,128)(2,1)S(1)} %bitcast.65, bf16[]{:T(256)} %broadcast.142), dimensions={1}, to_apply=%bitcast.61.reduce_sub_computation | reduce | bytes 2097154
  11.2 1.6 reshape.199
  12.8 10.5 %all-to-all-start = ((bf16[32,2,8192]{2,1,0:T(2,128)(2,1)}), bf16[32,2,8192]{2,1,0:T(2,128)(2,1)S(1)}, u32[]{:S(2)}, u32[]{:S(2)}) async-start(bf16[32,2,8192]{2,1,0:T(2,128)(2,1)} %reshape.199), calls=%async_computation | async-start | bytes 2097152 | tf_op jit(solution)/shard_map/all_to_all | solution.py:45
  23.4 1.3 dynamic-slice
  25.4 28.7 %all-reduce = s32[128]{0:T(128)S(1)} all-reduce(s32[128]{0:T(128)S(1)} %bitcast_dynamic-update-slice_fusion), channel_id=1, replica_groups=mesh['station'=32,'tm'=16] {'station'}, use_global_device_ids=true, to_apply=%add | all-reduce | flops 128 | bytes 1024
  54.2 0.6 gather_fusion.1
  55.1 19.2 %cosine_convert_fusion = (bf16[2048,512]{1,0:T(8,128)(2,1)}, bf16[2048,512]{1,0:T(8,128)(2,1)}) fusion(s32[512]{0:T(512)S(1)} %iota_add_fusion, s32[2048]{0:T(1024)S(1)} %multiply_add_fusion), kind=kLoop, calls=%fused_computation.15 | loop fusion | flops 17825792 | bytes 4204544 | tf_op jit(solution)/shard_map/convert.24
  74.3 1.1 reshape.200
  75.4 6.2 %bitcast_reduce_fusion = bf16[128,4096]{1,0:T(8,128)(2,1)S(1)} fusion(bf16[128,1,4096]{2,1,0:T(2,128)(2,1)S(1)} %reshape.200), kind=kLoop, calls=%fused_computation.51 | loop fusion | bytes 2097152 | tf_op jit(solution)/shard_map/all_to_all | solution.py:45
  81.6 0.4 reshape.167
  82.0 1.0 gather_fusion
  83.0 0.3 bitcast_select_fusion
  83.5 1.2 fusion.11
  84.7 1.2 concatenate.13
  85.8 1.1 concatenate.14
  87.0 0.9 copy-done
  87.8 3.6 %fusion.4 = f32[272,512]{1,0:T(8,128)S(1)} fusion(bf16[2048,512]{1,0:T(8,128)(2,1)} %get-tuple-element.12, bf16[2048,512]{1,0:T(8,128)(2,1)S(1)} %copy-done, bf16[272,2048]{1,0:T(8,128)(2,1)} %concatenate.14, bf16[272,2048]{1,0:T(8,128)(2,1)} %concatenate.13), kind=kOutput, calls=%fused_computation.10 | convolution fusion | flops 1153695744 | bytes 6979584 | tf_op jit(solution)/shard_map/dot_general | solution.py:59
  91.4 35.2 %fusion = f32[24,512]{1,0:T(8,128)S(1)} fusion(f32[272,512]{1,0:T(8,128)S(1)} %fusion.4), kind=kCustom, calls=%all-reduce-scatter | all-reduce-scatter fusion | flops 196609 | bytes 608256
  126.7 1.3 collective-permute-start.3
  128.0 7.0 %collective-permute-start.2 = (f32[24,512]{1,0:T(8,128)S(1)}, f32[24,512]{1,0:T(8,128)S(1)}, u32[]{:S(2)}, u32[]{:S(2)}) collective-permute-start(f32[24,512]{1,0:T(8,128)S(1)} %fusion), channel_id=1, source_target_pairs={{0,3},{1,4},{2,5},{3,6},{4,7},{5,8},{6,9},{7,10},{8,11},{9,12},{10... | collective-permute-start | bytes 147464
  135.0 1.3 collective-permute-start.1
  136.3 3.1 %collective-permute-start = (f32[24,512]{1,0:T(8,128)S(1)}, f32[24,512]{1,0:T(8,128)S(1)}, u32[]{:S(2)}, u32[]{:S(2)}) collective-permute-start(f32[24,512]{1,0:T(8,128)S(1)} %fusion), channel_id=1, source_target_pairs={{0,1},{1,2},{2,3},{3,4},{4,5},{5,6},{6,7},{7,8},{8,9},{9,10},{10,1... | collective-permute-start | bytes 147464
  139.4 1.7 collective-permute-start.4
  141.3 0.6 fusion.18
  143.2 23.6 %all-reduce.2 = f32[272]{0:T(512)S(1)} all-reduce(f32[272]{0:T(512)S(1)} %reshape.162), channel_id=3, replica_groups=mesh['station'=32,'tm'=16] {'tm'}, use_global_device_ids=true, to_apply=%region_1.2.clone | all-reduce | flops 272 | bytes 2176
  166.9 0.7 concatenate.17
  167.6 0.7 fusion.13
  (33 shorter events, 0.9 us)
Async XLA Ops:
  11.1 12.2 %copy-start.3 = (s32[1,17]{1,0:T(1,128)S(1)}, s32[1,17]{1,0:T(1,128)}, u32[]{:S(2)}) copy-start(s32[1,17]{1,0:T(1,128)} %param.5) | copy-start | bytes 208
  11.2 14.2 %copy-start.4 = (s32[1,4]{1,0:T(1,128)S(1)}, s32[1,4]{1,0:T(1,128)}, u32[]{:S(2)}) copy-start(s32[1,4]{1,0:T(1,128)} %param.4) | copy-start | bytes 52
  11.2 43.8 %copy-start.1 = (bf16[1,4,4096]{2,1,0:T(4,128)(2,1)S(1)}, bf16[1,4,4096]{2,1,0:T(4,128)(2,1)}, u32[]{:S(2)}) copy-start(bf16[1,4,4096]{2,1,0:T(4,128)(2,1)} %param.3) | copy-start | bytes 98308
  12.8 61.5 %all-to-all-start = ((bf16[32,2,8192]{2,1,0:T(2,128)(2,1)}), bf16[32,2,8192]{2,1,0:T(2,128)(2,1)S(1)}, u32[]{:S(2)}, u32[]{:S(2)}) async-start(bf16[32,2,8192]{2,1,0:T(2,128)(2,1)} %reshape.199), calls=%async_computation | async-start | bytes 2097152 | tf_op jit(solution)/shard_map/all_to_all | solution.py:45
  85.8 2.0 %copy-start = (bf16[2048,512]{1,0:T(8,128)(2,1)S(1)}, bf16[2048,512]{1,0:T(8,128)(2,1)}, u32[]{:S(2)}) copy-start(bf16[2048,512]{1,0:T(8,128)(2,1)} %get-tuple-element.11) | copy-start | bytes 6291460
  87.8 53.5 %copy-start.2 = (u32[512]{0:T(512)S(1)}, u32[512]{0:T(512)}, u32[]{:S(2)}) copy-start(u32[512]{0:T(512)} %constant.65) | copy-start | bytes 6148
  126.7 40.2 %collective-permute-start.3 = (f32[24,512]{1,0:T(8,128)S(1)}, f32[24,512]{1,0:T(8,128)S(1)}, u32[]{:S(2)}, u32[]{:S(2)}) collective-permute-start(f32[24,512]{1,0:T(8,128)S(1)} %fusion), channel_id=1, source_target_pairs={{0,4},{1,5},{2,6},{3,7},{4,8},{5,9},{6,10},{7,11},{8,12},{9,13},{1... | collective-permute-start | bytes 147464
  128.0 38.9 %collective-permute-start.2 = (f32[24,512]{1,0:T(8,128)S(1)}, f32[24,512]{1,0:T(8,128)S(1)}, u32[]{:S(2)}, u32[]{:S(2)}) collective-permute-start(f32[24,512]{1,0:T(8,128)S(1)} %fusion), channel_id=1, source_target_pairs={{0,3},{1,4},{2,5},{3,6},{4,7},{5,8},{6,9},{7,10},{8,11},{9,12},{10... | collective-permute-start | bytes 147464
  135.0 31.8 %collective-permute-start.1 = (f32[24,512]{1,0:T(8,128)S(1)}, f32[24,512]{1,0:T(8,128)S(1)}, u32[]{:S(2)}, u32[]{:S(2)}) collective-permute-start(f32[24,512]{1,0:T(8,128)S(1)} %fusion), channel_id=1, source_target_pairs={{0,2},{1,3},{2,4},{3,5},{4,6},{5,7},{6,8},{7,9},{8,10},{9,11},{10,... | collective-permute-start | bytes 147464
  136.3 30.6 %collective-permute-start = (f32[24,512]{1,0:T(8,128)S(1)}, f32[24,512]{1,0:T(8,128)S(1)}, u32[]{:S(2)}, u32[]{:S(2)}) collective-permute-start(f32[24,512]{1,0:T(8,128)S(1)} %fusion), channel_id=1, source_target_pairs={{0,1},{1,2},{2,3},{3,4},{4,5},{5,6},{6,7},{7,8},{8,9},{9,10},{10,1... | collective-permute-start | bytes 147464
  139.4 27.4 %collective-permute-start.4 = (f32[9,512]{1,0:T(8,128)S(1)}, f32[9,512]{1,0:T(8,128)S(1)}, u32[]{:S(2)}, u32[]{:S(2)}) collective-permute-start(f32[9,512]{1,0:T(8,128)S(1)} %slice.24), channel_id=1, source_target_pairs={{0,5},{1,6},{2,7},{3,8},{4,9},{5,10},{6,11},{7,12},{8,13},{9,14},{... | collective-permute-start | bytes 55304
